TPU v7x, 128 devices: a whole 4x4x4 slice. The times are simulated.
128 devices in a mesh: row: 8 (over y, core), col: 16 (over z, x).
Axes of the slice: x: 4, y: 4, z: 4, core: 2. Of those that a mesh axis runs over, the one named last changes fastest.
Arguments:
- wavefield: bfloat16 [65536, 2, 128], P(('col', 'row')), may hold values from -6 to 6
- recorded: bfloat16 [65536, 2, 128], P(('row', 'col')), may hold values from -6 to 6
- v_bases: bfloat16 [256, 256, 32, 256], P('row', 'col'), may hold values from -0.25 to 0.25
- u_bases: bfloat16 [256, 256, 32, 256], P(('row', 'col')), may hold values from -0.0625 to 0.0625
- ranks: int32 [256, 256], P('row', 'col'), may hold values from 1 to 16
Outputs:
- residual: float32 [65536, 2, 128], P(('row', 'col'))
- gradient: float32 [65536, 2, 128], P(('col', 'row'))
Inputs may be any that keep to these rules, and one draw needn't show every extreme that they name: `ranks`: some tile has rank 16.
All inputs are finite; a program needn't handle non-finite values.
Results may differ from a plain program's by a relative error of at most 0.0038.
Values may be sent and summed in bfloat16 or wider, within the bound.
No kernel may reach another device: no remote copies, remote signals or barrier semaphores. Data moves between devices by JAX's collectives and lax.ppermute only.
A program may use at most 128 MiB of HBM per device.

v0:
```python
import jax
import jax.numpy as jnp
from jax import lax
from jax.sharding import PartitionSpec as P


def combine_adjoint(prod):
    half = prod.shape[2] // 2
    real = prod[:, :, :half, 0] + prod[:, :, half:, 1]
    imag = prod[:, :, :half, 1] - prod[:, :, half:, 0]
    return jnp.stack([real, imag], axis=3)


def stacked(coeffs):
    real = coeffs[:, :, :, 0]
    imag = coeffs[:, :, :, 1]
    first = jnp.concatenate([real, -imag], axis=2)
    second = jnp.concatenate([imag, real], axis=2)
    return jnp.stack([first, second], axis=3)


def v_adjoint(bases, blocks, mask):
    prod = jnp.einsum("ijrk,jkcs->ijrcs", bases, blocks, preferred_element_type=jnp.float32)
    return (combine_adjoint(prod) * mask[:, :, :, None, None]).astype(jnp.bfloat16)


def u_apply(bases, coeffs):
    return jnp.einsum(
        "ijrk,ijrcs->ikcs", bases, stacked(coeffs), preferred_element_type=jnp.float32
    )


def u_adjoint(bases, rows):
    prod = jnp.einsum("ijrk,ikcs->ijrcs", bases, rows, preferred_element_type=jnp.float32)
    return combine_adjoint(prod).astype(jnp.bfloat16)


def v_apply(bases, back, mask):
    masked = back * mask.astype(jnp.bfloat16)[:, :, :, None, None]
    return jnp.einsum(
        "ijrk,ijrcs->jkcs", bases, stacked(masked), preferred_element_type=jnp.float32
    )


def body(wavefield, recorded, v_bases, u_bases, ranks):
    tile = v_bases.shape[3]
    rank = v_bases.shape[2] // 2
    sources = wavefield.shape[2]
    levels = lax.broadcasted_iota(jnp.int32, (ranks.shape[0], ranks.shape[1], rank), 2)
    mask = (levels < ranks[:, :, None]).astype(jnp.float32)
    gathered = lax.all_gather(wavefield, "row", axis=0, tiled=True)
    blocks = gathered.reshape(-1, tile, 2, sources)
    coeffs = v_adjoint(v_bases, blocks, mask)
    local_left = lax.all_to_all(u_bases, "col", split_axis=1, concat_axis=0, tiled=True)
    partial_value = u_apply(local_left, coeffs).reshape(-1, 2, sources)
    modelled = lax.psum_scatter(partial_value, "col", scatter_dimension=0, tiled=True)
    residual = modelled - recorded.astype(jnp.float32)
    rounded = residual.astype(jnp.bfloat16)
    whole_rows = lax.all_gather(rounded, "col", axis=0, tiled=True).reshape(-1, tile, 2, sources)
    back = u_adjoint(local_left, whole_rows)
    column_terms = v_apply(v_bases, back, mask)
    gradient = lax.psum_scatter(
        column_terms.reshape(-1, 2, sources), "row", scatter_dimension=0, tiled=True
    )
    return (residual, gradient)


def solution(mesh):
    in_specs = (
        P(("col", "row"), None, None),
        P(("row", "col"), None, None),
        P("row", "col", None, None),
        P(("row", "col"), None, None, None),
        P("row", "col"),
    )
    out_specs = (P(("row", "col"), None, None), P(("col", "row"), None, None))
    return jax.shard_map(body, mesh=mesh, in_specs=in_specs, out_specs=out_specs, check_vma=False)
```

profile of v0, /device:TPU:0, one launch (start us, length us, event | category | flops | bytes accessed | tf_op | source)
XLA Modules:
  0.0 404.6 jit_solution(17005958906156054134)
XLA Ops:
  7.2 8.1 %copy.35 = bf16[2,256,32,256]{3,2,0,1:T(8,128)(2,1)} copy(bf16[2,256,32,256]{3,2,1,0:T(8,128)(2,1)} %param.8) | data formatting | bytes 16777216 | tf_op args[3]
  15.2 0.0 copy-start
  15.2 0.0 copy-start.2
  15.2 8.2 %all-to-all-start = ((bf16[2,256,32,256]{3,2,0,1:T(8,128)(2,1)}), bf16[2,256,32,256]{3,2,0,1:T(8,128)(2,1)}, u32[]{:S(2)}, u32[]{:S(2)}) async-start(bf16[2,256,32,256]{3,2,0,1:T(8,128)(2,1)} %copy.35), calls=%async_computation | async-start | bytes 16777216 | tf_op jit(solution)/shard_map/all_to_all | solution.py:54
  23.4 0.0 all-gather.3.cloned.1.call-start
  23.5 0.0 copy-done
  23.5 0.7 copy.31
  24.2 0.0 all-gather.3.cloned.1.call-update
  24.2 0.0 reduce-scatter.3.cloned.1.call-start
  24.3 0.0 copy-done.2
  24.3 0.1 fusion.20
  24.4 29.1 %all-gather.3.cloned.1.call-done = bf16[4096,2,128]{2,0,1:T(8,128)(2,1)} async-done(((bf16[512,2,128]{2,0,1:T(8,128)(2,1)}), bf16[4096,2,128]{2,0,1:T(8,128)(2,1)}) %all-gather.3.cloned.1.call-update) | async-done | bytes 2097168 | tf_op jit(solution)/shard_map/all_gather | solution.py:51
  53.5 12.1 %convolution_bitcast_fusion.1 = f32[32,16,32,2,128]{4,2,0,3,1:T(8,128)} fusion(bf16[16,256,2,128,1]{3,1,0,2,4:T(8,128)(2,1)} %bitcast.69, bf16[32,16,32,256]{3,2,1,0:T(8,128)(2,1)} %param.7), kind=kOutput, calls=%fused_computation.1 | convolution fusion | flops 2147483648 | bytes 27262976 | tf_op jit(solution)/shard_map/ijrk,jkcs->ijrcs/dot_general | solution.py:23
  65.6 9.4 %slice_add_fusion.1 = (f32[32,16,16,1,128]{4,2,0,3,1:T(8,128)S(1)}, f32[32,16,16,1,128]{4,2,0,3,1:T(8,128)}) fusion(f32[32,16,32,2,128]{4,2,0,3,1:T(8,128)} %convolution_bitcast_fusion.1), kind=kLoop, calls=%fused_computation.17 | loop fusion | flops 2097152 | bytes 25165824 | tf_op jit(solution)/shard_map/add | solution.py:9
  75.0 3.8 fusion
  78.7 0.3 fusion.21
  79.0 1.1 slice_bitcast_fusion.2
  80.2 4.1 %maximum_bitcast_fusion = (bf16[32,16,32,1,128]{4,2,0,1,3:T(8,128)(2,1)}, bf16[32,16,32,1,128]{4,2,0,1,3:T(8,128)(2,1)}) fusion(bf16[32,16,16,128]{3,2,0,1:T(8,128)(2,1)S(1)} %fusion.21, bf16[32,16,16,128]{3,2,0,1:T(8,128)(2,1)S(1)} %get-tuple-element.15, bf16[32,16,16,128]{3,2,0,1:T(8,128)(2,1)S(1)} %get-tuple-element.14), kind=kLoop, calls=%fused_computation.18 | loop fusion | flops 16777216 | bytes 14680064 | tf_op jit(solution)/shard_map/stack | solution.py:19
  84.3 63.3 %all-to-all-done = bf16[2,256,32,256]{3,2,0,1:T(8,128)(2,1)} async-done(((bf16[2,256,32,256]{3,2,0,1:T(8,128)(2,1)}), bf16[2,256,32,256]{3,2,0,1:T(8,128)(2,1)}, u32[]{:S(2)}, u32[]{:S(2)}) %all-to-all-start) | async-done | bytes 8388640 | tf_op jit(solution)/shard_map/all_to_all | solution.py:54
  147.6 8.1 %copy.36 = bf16[2,16,16,32,256]{4,3,2,0,1:T(8,128)(2,1)} copy(bf16[2,16,16,32,256]{4,3,0,2,1:T(8,128)(2,1)} %bitcast.8) | data formatting | bytes 16777216 | tf_op jit(solution)/shard_map/all_to_all | solution.py:54
  155.6 11.5 %fusion.10 = f32[32,256,2,128]{1,3,2,0:T(8,128)} fusion(bf16[32,16,32,256,1]{3,2,1,4,0:T(8,128)(2,1)} %bitcast.64, bf16[32,16,32,1,128]{4,2,0,1,3:T(8,128)(2,1)} %get-tuple-element.19, bf16[32,16,32,1,128]{4,2,0,1,3:T(8,128)(2,1)} %get-tuple-element.18), kind=kOutput, calls=%fused_computation.24 | convolution fusion | flops 2151677952 | bytes 25165824 | tf_op jit(solution)/shard_map/ijrk,ijrcs->ikcs/dot_general | solution.py:28
  167.1 8.9 %copy.38 = f32[32,256,2,128]{3,1,0,2:T(8,128)} copy(f32[32,256,2,128]{1,3,2,0:T(8,128)} %fusion.10) | data formatting | bytes 16777216 | tf_op jit(solution)/shard_map/ijrk,ijrcs->ikcs/dot_general | solution.py:28
  176.0 0.0 copy-start.1
  176.0 0.0 reduce-scatter.3.cloned.1.call-update
  176.0 0.0 all-gather.5.cloned.1.call-start
  176.1 86.2 %reduce-scatter.3.cloned.1.call-done = f32[512,2,128]{2,0,1:T(8,128)} async-done(((f32[8192,2,128]{2,0,1:T(8,128)}), f32[512,2,128]{2,0,1:T(8,128)}) %reduce-scatter.3.cloned.1.call-update) | async-done | bytes 524304 | tf_op jit(solution)/shard_map/reduce_scatter | solution.py:56
  262.2 0.0 copy-done.1
  262.2 1.8 fusion.23
  264.1 0.0 all-gather.5.cloned.1.call-update
  264.1 0.2 reduce-scatter.5.cloned.1.call-start
  264.3 0.1 copy.41
  264.4 51.5 %all-gather.5.cloned.1.call-done = bf16[8192,2,128]{2,0,1:T(8,128)(2,1)} async-done(((bf16[512,2,128]{2,0,1:T(8,128)(2,1)}), bf16[8192,2,128]{2,0,1:T(8,128)(2,1)}) %all-gather.5.cloned.1.call-update) | async-done | bytes 4194320 | tf_op jit(solution)/shard_map/all_gather | solution.py:59
  315.8 12.7 %convolution_bitcast_fusion = f32[32,16,32,2,128]{4,2,1,3,0:T(8,128)} fusion(bf16[32,16,32,256,1]{3,2,1,4,0:T(8,128)(2,1)} %bitcast.65, bf16[32,256,2,128,1]{3,1,0,2,4:T(8,128)(2,1)} %bitcast.68), kind=kOutput, calls=%fused_computation | convolution fusion | flops 2147483648 | bytes 29360128 | tf_op jit(solution)/shard_map/ijrk,ikcs->ijrcs/dot_general | solution.py:34
  328.6 6.7 %fusion.8 = (bf16[32,16,16,1,128]{4,2,1,3,0:T(8,128)(2,1)S(1)}, bf16[32,16,16,1,128]{4,2,1,3,0:T(8,128)(2,1)S(1)}) fusion(f32[32,16,32,2,128]{4,2,1,3,0:T(8,128)} %convolution_bitcast_fusion), kind=kLoop, calls=%fused_computation.15 | loop fusion | flops 4194304 | bytes 20971520 | tf_op jit(solution)/shard_map/convert
  335.3 1.4 maximum_multiply_fusion.1
  336.7 1.3 slice_bitcast_fusion
  338.0 0.3 fusion.22
  338.3 4.2 %maximum_bitcast_fusion.2 = (bf16[32,16,32,1,128]{4,2,1,0,3:T(8,128)(2,1)}, bf16[32,16,32,1,128]{4,2,1,0,3:T(8,128)(2,1)}) fusion(bf16[32,16,16,128]{3,2,1,0:T(8,128)(2,1)S(1)} %fusion.22, bf16[32,16,16,128]{3,2,1,0:T(8,128)(2,1)S(1)} %get-tuple-element.13, bf16[32,16,16,128]{3,2,1,0:T(8,128)(2,1)S(1)} %get-tuple-element.12), kind=kLoop, calls=%fused_computation.21 | loop fusion | flops 16777216 | bytes 14680064 | tf_op jit(solution)/shard_map/stack | solution.py:19
  342.4 10.3 %fusion.13 = f32[16,256,2,128]{1,3,2,0:T(8,128)} fusion(bf16[32,16,32,1,128]{4,2,1,0,3:T(8,128)(2,1)} %get-tuple-element.17, bf16[32,16,32,1,128]{4,2,1,0,3:T(8,128)(2,1)} %get-tuple-element.16, bf16[32,16,32,256]{3,2,1,0:T(8,128)(2,1)} %param.7), kind=kOutput, calls=%fused_computation.25 | convolution fusion | flops 2151677952 | bytes 20971520 | tf_op jit(solution)/shard_map/ijrk,ijrcs->jkcs/dot_general | solution.py:40
  352.7 5.4 %copy.45 = f32[16,256,2,128]{3,1,0,2:T(8,128)} copy(f32[16,256,2,128]{1,3,2,0:T(8,128)} %fusion.13) | data formatting | bytes 8388608 | tf_op jit(solution)/shard_map/ijrk,ijrcs->jkcs/dot_general | solution.py:40
  358.1 0.0 reduce-scatter.5.cloned.1.call-update
  358.1 1.2 copy.46
  359.3 36.5 %reduce-scatter.5.cloned.1.call-done = f32[512,2,128]{2,0,1:T(8,128)} async-done(((f32[4096,2,128]{2,0,1:T(8,128)}), f32[512,2,128]{2,0,1:T(8,128)}) %reduce-scatter.5.cloned.1.call-update) | async-done | bytes 524304 | tf_op jit(solution)/shard_map/reduce_scatter | solution.py:62
  395.9 2.2 copy.47
Async XLA Ops:
  15.2 8.2 %copy-start = (bf16[512,2,128]{2,1,0:T(2,128)(2,1)S(1)}, bf16[512,2,128]{2,1,0:T(2,128)(2,1)}, u32[]{:S(2)}) copy-start(bf16[512,2,128]{2,1,0:T(2,128)(2,1)} %param.5) | copy-start | bytes 786436
  15.2 9.1 %copy-start.2 = (s32[32,16]{0,1:T(8,128)S(1)}, s32[32,16]{0,1:T(8,128)}, u32[]{:S(2)}) copy-start(s32[32,16]{0,1:T(8,128)} %param.9) | copy-start | bytes 6148
  15.2 132.3 %all-to-all-start = ((bf16[2,256,32,256]{3,2,0,1:T(8,128)(2,1)}), bf16[2,256,32,256]{3,2,0,1:T(8,128)(2,1)}, u32[]{:S(2)}, u32[]{:S(2)}) async-start(bf16[2,256,32,256]{3,2,0,1:T(8,128)(2,1)} %copy.35), calls=%async_computation | async-start | bytes 16777216 | tf_op jit(solution)/shard_map/all_to_all | solution.py:54
  23.4 30.1 %all-gather.3.cloned.1.call-start = ((), (), s32[]{:S(2)}) async-start(), calls=%async_computation.3 | async-start | bytes 2359296 | tf_op jit(solution)/shard_map/all_gather | solution.py:51
  24.2 238.0 %reduce-scatter.3.cloned.1.call-start = ((), (), s32[]{:S(2)}) async-start(), calls=%async_computation.4 | async-start | bytes 8912896 | tf_op jit(solution)/shard_map/reduce_scatter | solution.py:56
  176.0 86.2 %copy-start.1 = (bf16[512,2,128]{2,1,0:T(2,128)(2,1)S(1)}, bf16[512,2,128]{2,1,0:T(2,128)(2,1)}, u32[]{:S(2)}) copy-start(bf16[512,2,128]{2,1,0:T(2,128)(2,1)} %param.6) | copy-start | bytes 786436
  176.0 139.8 %all-gather.5.cloned.1.call-start = ((), (), s32[]{:S(2)}) async-start(), calls=%async_computation.5 | async-start | bytes 4456448 | tf_op jit(solution)/shard_map/all_gather | solution.py:59
  264.1 131.8 %reduce-scatter.5.cloned.1.call-start = ((), (), s32[]{:S(2)}) async-start(), calls=%async_computation.6 | async-start | bytes 4718592 | tf_op jit(solution)/shard_map/reduce_scatter | solution.py:62
Sparse Core Ops, SparseCore 0:
  26.5 26.9 all-gather.2
  176.2 86.0 reduce-scatter.2
  265.0 50.8 all-gather.4
  358.3 37.5 reduce-scatter.4
where the time goes:
time: 405 us
  waiting for transfers between devices  267 us (66%)
  matrix products  46.6 us (12%)
  local copies, waits for them, and re-layouts  37.1 us (9%)
  other arithmetic  32 us (8%)
  between operations  13.9 us (3%)
  starting transfers between devices  8.52 us (2%)
    reduce_scatter x1, waiting for transfers between devices, body(): lax.psum_scatter(partial_value, 'col', scatter_dimension=0, tiled=True)  86.2 us
    all_to_all x1, waiting for transfers between devices, body(): lax.all_to_all(u_bases, 'col', split_axis=1, concat_axis=0, tiled=True)  63.3 us
    all_gather x1, waiting for transfers between devices, body(): lax.all_gather(rounded, 'col', axis=0, tiled=True)  51.5 us
    reduce_scatter x1, waiting for transfers between devices, body(): lax.psum_scatter(column_terms.reshape(-1, 2, sources), 'row', scatter_dim...  36.5 us
    all_gather x1, waiting for transfers between devices, body(): gathered = lax.all_gather(wavefield, 'row', axis=0, tiled=True)  29.1 us
    dot_general x1, matrix products, u_adjoint(): jnp.einsum('ijrk,ikcs->ijrcs', bases, rows, preferred_element_type=jnp.fl...  12.7 us
    unnamed x10, local copies, waits for them, and re-layouts  12.3 us
    dot_general x1, matrix products, v_adjoint(): jnp.einsum('ijrk,jkcs->ijrcs', bases, blocks, preferred_element_type=jnp....  12.1 us
  transfers between devices with their start and end apart: 5, of which 5 were waited for; matrix products, arithmetic and copies ran while one was open for 8% of the time, Pallas kernels for 0%

commit v1 on v0

--- a/solution.py
+++ b/solution.py
@@ -56,7 +56,9 @@
     modelled = lax.psum_scatter(partial_value, "col", scatter_dimension=0, tiled=True)
     residual = modelled - recorded.astype(jnp.float32)
     rounded = residual.astype(jnp.bfloat16)
-    whole_rows = lax.all_gather(rounded, "col", axis=0, tiled=True).reshape(-1, tile, 2, sources)
+    whole_rows = jnp.concatenate(
+        lax.all_to_all(jnp.stack([rounded] * lax.axis_size("col")), "col", 0, 0), axis=0
+    ).reshape(-1, tile, 2, sources)
     back = u_adjoint(local_left, whole_rows)
     column_terms = v_apply(v_bases, back, mask)
     gradient = lax.psum_scatter(

time: 405 us -> 424 us (1.047)
  local copies, waits for them, and re-layouts: 37.1 us -> 44.7 us
  waiting for transfers between devices: 267 us -> 273 us
  starting transfers between devices: 8.52 us -> 13.4 us
    all_to_all x0 -> x1, waiting for transfers between devices: none -> 59 us  [body(): lax.all_to_all(jnp.stack([rounded] * lax.axis_size('col')), 'col', 0, 0)]
    all_gather x1 -> x0, waiting for transfers between devices: 51.5 us -> none  [body(): lax.all_gather(rounded, 'col', axis=0, tiled=True)]
    all_to_all x0 -> x1, starting transfers between devices: none -> 4.96 us  [body(): lax.all_to_all(jnp.stack([rounded] * lax.axis_size('col')), 'col', 0, 0)]
    all_to_all x0 -> x1, local copies, waits for them, and re-layouts: none -> 4.61 us  [body(): lax.all_to_all(jnp.stack([rounded] * lax.axis_size('col')), 'col', 0, 0)]
where the time goes in v1:
time: 424 us; the launch traced here: 423 us
  waiting for transfers between devices  273 us (64%)
  matrix products  46.7 us (11%)
  local copies, waits for them, and re-layouts  44.7 us (11%)
  other arithmetic  31.2 us (7%)
  between operations  13.9 us (3%)
  starting transfers between devices  13.4 us (3%)
    reduce_scatter x1, waiting for transfers between devices, body(): lax.psum_scatter(partial_value, 'col', scatter_dimension=0, tiled=True)  86.3 us
    all_to_all x1, waiting for transfers between devices, body(): lax.all_to_all(u_bases, 'col', split_axis=1, concat_axis=0, tiled=True)  63.3 us
    all_to_all x1, waiting for transfers between devices, body(): lax.all_to_all(jnp.stack([rounded] * lax.axis_size('col')), 'col', 0, 0)  59 us
    reduce_scatter x1, waiting for transfers between devices, body(): lax.psum_scatter(column_terms.reshape(-1, 2, sources), 'row', scatter_dim...  35.4 us
    all_gather x1, waiting for transfers between devices, body(): gathered = lax.all_gather(wavefield, 'row', axis=0, tiled=True)  29.1 us
    dot_general x1, matrix products, u_adjoint(): jnp.einsum('ijrk,ikcs->ijrcs', bases, rows, preferred_element_type=jnp.fl...  12.7 us
    unnamed x10, local copies, waits for them, and re-layouts  12.3 us
    dot_general x1, matrix products, v_adjoint(): jnp.einsum('ijrk,jkcs->ijrcs', bases, blocks, preferred_element_type=jnp....  12.1 us
  transfers between devices with their start and end apart: 5, of which 5 were waited for; matrix products, arithmetic and copies ran while one was open for 8% of the time, Pallas kernels for 0%

profile of v1, /device:TPU:0, one launch (start us, length us, event | category | flops | bytes accessed | tf_op | source)
XLA Modules:
  0.0 422.9 jit_solution(13142162256562012293)
XLA Ops:
  7.2 8.1 %copy.35 = bf16[2,256,32,256]{3,2,0,1:T(8,128)(2,1)} copy(bf16[2,256,32,256]{3,2,1,0:T(8,128)(2,1)} %param.8) | data formatting | bytes 16777216 | tf_op args[3]
  15.2 0.0 copy-start
  15.2 0.0 copy-start.2
  15.2 8.2 %all-to-all-start = ((bf16[2,256,32,256]{3,2,0,1:T(8,128)(2,1)}), bf16[2,256,32,256]{3,2,0,1:T(8,128)(2,1)}, u32[]{:S(2)}, u32[]{:S(2)}) async-start(bf16[2,256,32,256]{3,2,0,1:T(8,128)(2,1)} %copy.35), calls=%async_computation | async-start | bytes 16777216 | tf_op jit(solution)/shard_map/all_to_all | solution.py:54
  23.4 0.0 all-gather.2.cloned.1.call-start
  23.5 0.0 copy-done
  23.5 0.7 copy.31
  24.2 0.0 all-gather.2.cloned.1.call-update
  24.2 0.0 reduce-scatter.3.cloned.1.call-start
  24.3 0.0 copy-done.2
  24.3 0.1 fusion.20
  24.4 29.1 %all-gather.2.cloned.1.call-done = bf16[4096,2,128]{2,0,1:T(8,128)(2,1)} async-done(((bf16[512,2,128]{2,0,1:T(8,128)(2,1)}), bf16[4096,2,128]{2,0,1:T(8,128)(2,1)}) %all-gather.2.cloned.1.call-update) | async-done | bytes 2097168 | tf_op jit(solution)/shard_map/all_gather | solution.py:51
  53.5 12.1 %convolution_bitcast_fusion.1 = f32[32,16,32,2,128]{4,2,0,3,1:T(8,128)} fusion(bf16[16,256,2,128,1]{3,1,0,2,4:T(8,128)(2,1)} %bitcast.69, bf16[32,16,32,256]{3,2,1,0:T(8,128)(2,1)} %param.7), kind=kOutput, calls=%fused_computation.1 | convolution fusion | flops 2147483648 | bytes 27262976 | tf_op jit(solution)/shard_map/ijrk,jkcs->ijrcs/dot_general | solution.py:23
  65.6 9.4 %slice_add_fusion.1 = (f32[32,16,16,1,128]{4,2,0,3,1:T(8,128)S(1)}, f32[32,16,16,1,128]{4,2,0,3,1:T(8,128)}) fusion(f32[32,16,32,2,128]{4,2,0,3,1:T(8,128)} %convolution_bitcast_fusion.1), kind=kLoop, calls=%fused_computation.17 | loop fusion | flops 2097152 | bytes 25165824 | tf_op jit(solution)/shard_map/add | solution.py:9
  75.0 3.8 fusion
  78.8 0.3 fusion.21
  79.0 1.1 slice_bitcast_fusion.2
  80.2 4.1 maximum_bitcast_fusion
  84.3 63.3 %all-to-all-done = bf16[2,256,32,256]{3,2,0,1:T(8,128)(2,1)} async-done(((bf16[2,256,32,256]{3,2,0,1:T(8,128)(2,1)}), bf16[2,256,32,256]{3,2,0,1:T(8,128)(2,1)}, u32[]{:S(2)}, u32[]{:S(2)}) %all-to-all-start) | async-done | bytes 8388640 | tf_op jit(solution)/shard_map/all_to_all | solution.py:54
  147.6 8.1 %copy.36 = bf16[2,16,16,32,256]{4,3,2,0,1:T(8,128)(2,1)} copy(bf16[2,16,16,32,256]{4,3,0,2,1:T(8,128)(2,1)} %bitcast.8) | data formatting | bytes 16777216 | tf_op jit(solution)/shard_map/all_to_all | solution.py:54
  155.6 11.5 %fusion.10 = f32[32,256,2,128]{1,3,2,0:T(8,128)} fusion(bf16[32,16,32,256,1]{3,2,1,4,0:T(8,128)(2,1)} %bitcast.64, bf16[32,16,32,1,128]{4,2,0,1,3:T(8,128)(2,1)} %get-tuple-element.19, bf16[32,16,32,1,128]{4,2,0,1,3:T(8,128)(2,1)} %get-tuple-element.18), kind=kOutput, calls=%fused_computation.24 | convolution fusion | flops 2151677952 | bytes 25165824 | tf_op jit(solution)/shard_map/ijrk,ijrcs->ikcs/dot_general | solution.py:28
  167.1 8.9 %copy.38 = f32[32,256,2,128]{3,1,0,2:T(8,128)} copy(f32[32,256,2,128]{1,3,2,0:T(8,128)} %fusion.10) | data formatting | bytes 16777216 | tf_op jit(solution)/shard_map/ijrk,ijrcs->ikcs/dot_general | solution.py:28
  176.0 0.0 copy-start.1
  176.0 0.0 reduce-scatter.3.cloned.1.call-update
  176.1 86.3 %reduce-scatter.3.cloned.1.call-done = f32[512,2,128]{2,0,1:T(8,128)} async-done(((f32[8192,2,128]{2,0,1:T(8,128)}), f32[512,2,128]{2,0,1:T(8,128)}) %reduce-scatter.3.cloned.1.call-update) | async-done | bytes 524304 | tf_op jit(solution)/shard_map/reduce_scatter | solution.py:56
  262.3 0.0 copy-done.1
  262.3 1.1 fusion.23
  263.4 2.9 stack.23
  266.4 5.0 %all-to-all-start.1 = ((bf16[16,512,2,128]{3,1,2,0:T(8,128)(2,1)}), bf16[16,512,2,128]{3,1,2,0:T(8,128)(2,1)}, u32[]{:S(2)}, u32[]{:S(2)}) async-start(bf16[16,512,2,128]{3,1,2,0:T(8,128)(2,1)} %stack.23), calls=%async_computation.2 | async-start | bytes 8388608 | tf_op jit(solution)/shard_map/all_to_all | solution.py:60
  271.3 0.2 reduce-scatter.5.cloned.1.call-start
  271.6 0.1 copy.42
  271.6 59.0 %all-to-all-done.1 = bf16[16,512,2,128]{3,1,2,0:T(8,128)(2,1)} async-done(((bf16[16,512,2,128]{3,1,2,0:T(8,128)(2,1)}), bf16[16,512,2,128]{3,1,2,0:T(8,128)(2,1)}, u32[]{:S(2)}, u32[]{:S(2)}) %all-to-all-start.1) | async-done | bytes 4194336 | tf_op jit(solution)/shard_map/all_to_all | solution.py:60
  330.6 4.6 %copy.40 = bf16[16,512,2,128]{3,1,0,2:T(8,128)(2,1)} copy(bf16[16,512,2,128]{3,1,2,0:T(8,128)(2,1)} %all-to-all-done.1) | data formatting | bytes 8388608 | tf_op jit(solution)/shard_map/all_to_all | solution.py:60
  335.2 12.7 %convolution_bitcast_fusion = f32[32,16,32,2,128]{4,2,1,3,0:T(8,128)} fusion(bf16[32,16,32,256,1]{3,2,1,4,0:T(8,128)(2,1)} %bitcast.65, bf16[32,256,2,128,1]{3,1,0,2,4:T(8,128)(2,1)} %bitcast.67), kind=kOutput, calls=%fused_computation | convolution fusion | flops 2147483648 | bytes 29360128 | tf_op jit(solution)/shard_map/ijrk,ikcs->ijrcs/dot_general | solution.py:34
  348.0 6.7 %fusion.8 = (bf16[32,16,16,1,128]{4,2,1,3,0:T(8,128)(2,1)S(1)}, bf16[32,16,16,1,128]{4,2,1,3,0:T(8,128)(2,1)S(1)}) fusion(f32[32,16,32,2,128]{4,2,1,3,0:T(8,128)} %convolution_bitcast_fusion), kind=kLoop, calls=%fused_computation.15 | loop fusion | flops 4194304 | bytes 20971520 | tf_op jit(solution)/shard_map/convert
  354.7 1.4 maximum_multiply_fusion.1
  356.1 1.3 slice_bitcast_fusion
  357.4 0.3 fusion.22
  357.7 4.2 maximum_bitcast_fusion.2
  361.8 10.3 %fusion.13 = f32[16,256,2,128]{1,3,2,0:T(8,128)} fusion(bf16[32,16,32,1,128]{4,2,1,0,3:T(8,128)(2,1)} %get-tuple-element.17, bf16[32,16,32,1,128]{4,2,1,0,3:T(8,128)(2,1)} %get-tuple-element.16, bf16[32,16,32,256]{3,2,1,0:T(8,128)(2,1)} %param.7), kind=kOutput, calls=%fused_computation.25 | convolution fusion | flops 2151677952 | bytes 20971520 | tf_op jit(solution)/shard_map/ijrk,ijrcs->jkcs/dot_general | solution.py:40
  372.1 5.4 %copy.46 = f32[16,256,2,128]{3,1,0,2:T(8,128)} copy(f32[16,256,2,128]{1,3,2,0:T(8,128)} %fusion.13) | data formatting | bytes 8388608 | tf_op jit(solution)/shard_map/ijrk,ijrcs->jkcs/dot_general | solution.py:40
  377.5 0.0 reduce-scatter.5.cloned.1.call-update
  377.6 1.2 copy.47
  378.8 35.4 %reduce-scatter.5.cloned.1.call-done = f32[512,2,128]{2,0,1:T(8,128)} async-done(((f32[4096,2,128]{2,0,1:T(8,128)}), f32[512,2,128]{2,0,1:T(8,128)}) %reduce-scatter.5.cloned.1.call-update) | async-done | bytes 524304 | tf_op jit(solution)/shard_map/reduce_scatter | solution.py:64
  414.2 2.2 copy.48
Async XLA Ops:
  15.2 8.2 %copy-start = (bf16[512,2,128]{2,1,0:T(2,128)(2,1)S(1)}, bf16[512,2,128]{2,1,0:T(2,128)(2,1)}, u32[]{:S(2)}) copy-start(bf16[512,2,128]{2,1,0:T(2,128)(2,1)} %param.5) | copy-start | bytes 786436
  15.2 9.1 %copy-start.2 = (s32[32,16]{0,1:T(8,128)S(1)}, s32[32,16]{0,1:T(8,128)}, u32[]{:S(2)}) copy-start(s32[32,16]{0,1:T(8,128)} %param.9) | copy-start | bytes 6148
  15.2 132.3 %all-to-all-start = ((bf16[2,256,32,256]{3,2,0,1:T(8,128)(2,1)}), bf16[2,256,32,256]{3,2,0,1:T(8,128)(2,1)}, u32[]{:S(2)}, u32[]{:S(2)}) async-start(bf16[2,256,32,256]{3,2,0,1:T(8,128)(2,1)} %copy.35), calls=%async_computation | async-start | bytes 16777216 | tf_op jit(solution)/shard_map/all_to_all | solution.py:54
  23.4 30.1 %all-gather.2.cloned.1.call-start = ((), (), s32[]{:S(2)}) async-start(), calls=%async_computation.4 | async-start | bytes 2359296 | tf_op jit(solution)/shard_map/all_gather | solution.py:51
  24.2 238.1 %reduce-scatter.3.cloned.1.call-start = ((), (), s32[]{:S(2)}) async-start(), calls=%async_computation.5 | async-start | bytes 8912896 | tf_op jit(solution)/shard_map/reduce_scatter | solution.py:56
  176.0 86.3 %copy-start.1 = (bf16[512,2,128]{2,1,0:T(2,128)(2,1)S(1)}, bf16[512,2,128]{2,1,0:T(2,128)(2,1)}, u32[]{:S(2)}) copy-start(bf16[512,2,128]{2,1,0:T(2,128)(2,1)} %param.6) | copy-start | bytes 786436
  266.4 64.3 %all-to-all-start.1 = ((bf16[16,512,2,128]{3,1,2,0:T(8,128)(2,1)}), bf16[16,512,2,128]{3,1,2,0:T(8,128)(2,1)}, u32[]{:S(2)}, u32[]{:S(2)}) async-start(bf16[16,512,2,128]{3,1,2,0:T(8,128)(2,1)} %stack.23), calls=%async_computation.2 | async-start | bytes 8388608 | tf_op jit(solution)/shard_map/all_to_all | solution.py:60
  271.3 142.8 %reduce-scatter.5.cloned.1.call-start = ((), (), s32[]{:S(2)}) async-start(), calls=%async_computation.6 | async-start | bytes 4718592 | tf_op jit(solution)/shard_map/reduce_scatter | solution.py:64
Sparse Core Ops, SparseCore 0:
  26.5 26.9 all-gather.1
  176.2 86.0 reduce-scatter.2
  377.7 36.4 reduce-scatter.4
